TPU v7x, 32 devices: a whole 2x2x4 slice. The times are simulated.
32 devices in a mesh: depth: 4 (over y, x), xline: 8 (over z, core).
Axes of the slice: x: 2, y: 2, z: 4, core: 2. Of those that a mesh axis runs over, the one named last changes fastest.
Arguments:
- receiver_data: bfloat16 [4, 2, 1024, 1024], P(None, None, None, 'xline'), may hold values from -6 to 6
- source_amp: bfloat16 [4, 2, 256], replicated, may hold values from -6 to 6
- source_x: int32 [256], replicated, may hold values from 0 to 1023
- source_y: int32 [256], replicated, may hold values from 0 to 1023
- omegas: float32 [4], replicated, may hold values from 0.5 to 3
- slowness: float32 [4, 1024, 1024], P('depth', None, 'xline'), may hold values from 0.2 to 2
- inverses: bfloat16 [4, 4, 2, 256, 256], replicated, may hold values from -0.1875 to 0.1875
- zones_x: int32 [4, 4], P('depth'), may hold values from 0 to 3
- zones_y: int32 [4, 4], P('depth'), may hold values from 0 to 3
Outputs:
- gradient: float32 [4, 1024, 1024], P('depth', None, 'xline')
All inputs are finite; a program needn't handle non-finite values.
Results may differ from a plain program's by a relative error of at most 0.015.
Values may be sent and summed in bfloat16 or wider, within the bound.
A program may use at most 64 MiB of HBM per device.

v0:
```python
import functools
import math

import jax
import jax.numpy as jnp
import numpy as np
from jax import lax
from jax.experimental import pallas as pl
from jax.experimental.pallas import tpu as pltpu
from jax.sharding import PartitionSpec as P

MESH = pl.DeviceIdType.MESH
F32 = jnp.float32
BF16 = jnp.bfloat16

SLOW_LOW, SLOW_HIGH = 0.2, 2.0
OMEGA_LOW, OMEGA_HIGH = 0.5, 3.0
SLOW_MID = 0.5 * (SLOW_LOW + SLOW_HIGH)
CODE_STEP = (SLOW_HIGH - SLOW_LOW) / 65532.0
HALF_SPAN = 0.5 * max(OMEGA_HIGH * SLOW_HIGH - math.pi, math.pi - OMEGA_LOW * SLOW_LOW) + 0.01


def fitted(function, count):
    nodes = np.cos(np.pi * (np.arange(64) + 0.5) / 64)
    square = 0.5 * HALF_SPAN**2 * (nodes + 1.0)
    fit = np.polynomial.Chebyshev.fit(square, function(np.sqrt(square)), count - 1)
    return [float(term) for term in fit.convert(kind=np.polynomial.Polynomial).coef]


ROOT2 = math.sqrt(2.0)
SIN_TERMS = fitted(lambda t: ROOT2 * np.sin(t) / t, 5)
COS_TERMS = fitted(lambda t: -ROOT2 * np.cos(t), 5)


def series(square, terms):
    total = square * terms[-1] + terms[-2]
    for term in terms[-3::-1]:
        total = total * square + term
    return total


def sincos(half):
    square = half * half
    root_sine = series(square, SIN_TERMS) * half
    return root_sine * series(square, COS_TERMS), root_sine * root_sine - 1.0


def block_form(blocks):
    k_real, k_imag = blocks[0], blocks[1]
    top = jnp.concatenate([k_real, -k_imag], axis=1)
    bottom = jnp.concatenate([k_imag, k_real], axis=1)
    return jnp.concatenate([top, bottom], axis=0)


def kernel(
    sections, pair, rows, recv_in, amp, src_x, src_y, omegas, slow_in, table_in,
    zones_x, zones_y,
    out, slow, slow_raw, code, rec, wave, table, zones, zone_buf, zone_rows, trig, rotated, inline,
    own, sent, got, total,
    local_sems, zone_send, zone_recv, slow_send, slow_recv, fwd_send, fwd_recv,
    rec_send, rec_recv, swap_send, swap_recv, grad_send, grad_recv,
):
    d = lax.axis_index("depth")
    line = lax.axis_index("xline")
    q = lax.rem(line, pair)
    block = line // pair
    mate_line = line + 1 - 2 * q
    width = recv_in.shape[3]
    order = pair * width
    slots = wave.shape[0]
    mine = pl.ds(pl.multiple_of(q * width, width), width)
    theirs = pl.ds(pl.multiple_of((1 - q) * width, width), width)

    def rows_of(section):
        return pl.ds(pl.multiple_of(section * order, order), order)

    barrier = pltpu.get_barrier_semaphore()
    pl.semaphore_signal(barrier, inc=1, device_id=(d, mate_line), device_id_type=MESH)
    others = [lax.rem(d + k, sections) for k in range(1, sections)]
    for other in others:
        pl.semaphore_signal(barrier, inc=1, device_id=(other, line), device_id_type=MESH)

    freqs = pl.ds(q * slots, slots)
    local = [
        pltpu.make_async_copy(
            slow_in.at[0], slow_raw, local_sems.at[0]
        ),
        pltpu.make_async_copy(
            recv_in.at[freqs, :, rows_of(d), :], rec.at[:, :, :, mine], local_sems.at[1]
        ),
        pltpu.make_async_copy(table_in.at[freqs], table, local_sems.at[2]),
    ]
    for copy in local:
        copy.start()
    zones[...] = jnp.zeros_like(zones)
    zones[0:1, 0:zones_x.shape[1]] = zones_x[...]
    zones[1:2, 0:zones_y.shape[1]] = zones_y[...]
    zone_buf[d] = zones[...]
    local[0].wait()
    for start in range(0, slow_raw.shape[0], order):
        part = slice(start, start + order)
        scaled = (slow_raw[part, :] - SLOW_MID) * (1.0 / CODE_STEP)
        code[part, :] = jnp.round(scaled).astype(jnp.int32).astype(jnp.int16)
    slow[d, :, mine] = code[rows_of(d), :]
    pl.semaphore_wait(barrier, sections)

    zone_copies, slow_copies = [], []
    for k, other in enumerate(others):
        zone_copies.append(
            pltpu.make_async_remote_copy(
                src_ref=zones, dst_ref=zone_buf.at[d], send_sem=zone_send.at[k],
                recv_sem=zone_recv.at[d], device_id=(other, line), device_id_type=MESH,
            )
        )
        slow_copies.append(
            pltpu.make_async_remote_copy(
                src_ref=code.at[rows_of(other), :], dst_ref=slow.at[d, :, mine],
                send_sem=slow_send.at[k], recv_sem=slow_recv.at[d],
                device_id=(other, line), device_id_type=MESH,
            )
        )
    for copy in zone_copies + slow_copies:
        copy.start()
    rec_copy = pltpu.make_async_remote_copy(
        src_ref=recv_in.at[pl.ds((1 - q) * slots, slots), :, rows_of(d), :],
        dst_ref=rec.at[:, :, :, mine], send_sem=rec_send, recv_sem=rec_recv,
        device_id=(d, mate_line), device_id_type=MESH,
    )
    rec_copy.start()

    def arrived_slow(level):
        return pltpu.make_async_remote_copy(
            src_ref=slow.at[level, :, mine], dst_ref=slow.at[level, :, mine],
            send_sem=slow_send.at[0], recv_sem=slow_recv.at[level],
            device_id=(d, mate_line), device_id_type=MESH,
        )

    def forward(level, half):
        return pltpu.make_async_remote_copy(
            src_ref=slow.at[level, :, half], dst_ref=slow.at[level, :, half],
            send_sem=fwd_send.at[level], recv_sem=fwd_recv.at[level],
            device_id=(d, mate_line), device_id_type=MESH,
        )

    def turn(level, lanes):
        for slot in range(slots):
            omega = omegas[q * slots + slot]
            slope = omega * (0.5 * CODE_STEP)
            shift = omega * (0.5 * SLOW_MID) - 0.5 * math.pi
            for start in range(0, order, rows):
                part = slice(start, start + rows)
                value = slow[level, part, lanes].astype(jnp.int32).astype(F32)
                sine, cosine = sincos(value * slope + shift)
                trig[level, slot, 0, part, lanes] = sine
                trig[level, slot, 1, part, lanes] = cosine

    forward(d, mine).start()

    points = src_x.shape[1]
    cells = lax.broadcasted_iota(jnp.int32, (order, points), 0)
    hit_x = cells + d * order == src_x[...]
    hit_y = jnp.where(cells + block * order == src_y[...], 1.0, 0.0).astype(BF16)
    for slot in range(slots):
        for part in range(2):
            amps = amp[q * slots + slot, pl.ds(part, 1), :].astype(F32)
            spread = jnp.where(hit_x, amps, 0.0).astype(BF16)
            field = lax.dot_general(
                spread, hit_y, (((1,), (1,)), ((), ())), preferred_element_type=F32
            )
            wave[slot, 0, part] = field.astype(BF16)

    local[1].wait()
    rec_copy.wait_recv()
    for slot in range(slots):
        wave[slot, 1, 0] = rec[slot, 0]
        wave[slot, 1, 1] = -rec[slot, 1]
    local[2].wait()
    forward(d, theirs).wait_recv()
    turn(d, slice(0, order))
    for level in range(sections):
        @pl.when(level != d)
        def _():
            pltpu.make_async_remote_copy(
                src_ref=zones, dst_ref=zone_buf.at[level], send_sem=zone_send.at[0],
                recv_sem=zone_recv.at[level], device_id=(d, mate_line), device_id_type=MESH,
            ).wait_recv()
    zone_copy = pltpu.make_async_copy(zone_buf, zone_rows, local_sems.at[3])
    zone_copy.start()
    zone_copy.wait()

    @pl.when(d != 0)
    def _():
        arrived_slow(0).wait_recv()
        forward(0, mine).start()
        turn(0, mine)
        forward(0, theirs).wait_recv()
        turn(0, theirs)

    def rotate(level, slot):
        for start in range(0, order, rows):
            part = slice(start, start + rows)
            sine, cosine = trig[level, slot, 0, part, :], trig[level, slot, 1, part, :]
            for field in range(2):
                real = wave[slot, field, 0, part, :].astype(F32)
                imag = wave[slot, field, 1, part, :].astype(F32)
                lanes = slice(field * order, (field + 1) * order)
                rotated[slot, part, lanes] = (real * cosine - imag * sine).astype(BF16)
                rotated[slot, order + start:order + start + rows, lanes] = (
                    real * sine + imag * cosine
                ).astype(BF16)

    def solve_inline(level, slot):
        m_x = block_form(table[slot, zone_rows[level, 0, d]])
        for field in range(2):
            lanes = slice(field * order, (field + 1) * order)
            value = rotated[slot, :, lanes]
            solved = value.astype(F32) + jnp.dot(m_x, value, preferred_element_type=F32)
            solved = solved.astype(BF16)
            inline[slot, lanes, 0:order] = solved[:order]
            inline[slot, lanes, order:] = solved[order:]

    def solve_crossline(level, slot):
        omega = omegas[q * slots + slot]
        m_y = block_form(table[slot, zone_rows[level, 1, block]])
        value = inline[slot]
        product = []
        for part in range(2):
            lanes = slice(part * order, (part + 1) * order)
            solved = value[:, lanes].astype(F32) + lax.dot_general(
                value, m_y[lanes], (((1,), (1,)), ((), ())), preferred_element_type=F32
            )
            product.append(solved[:order] * solved[order:])
            if level + 1 < sections:
                wave[slot, 0, part] = solved[:order].astype(BF16)
                wave[slot, 1, part] = solved[order:].astype(BF16)
        image = (omega * omega) * (product[0] - product[1])
        if slot == 0:
            total[...] = image
        else:
            total[...] += image

    def swap(level):
        return pltpu.make_async_remote_copy(
            src_ref=sent.at[level], dst_ref=got.at[level],
            send_sem=swap_send.at[level], recv_sem=swap_recv.at[level],
            device_id=(d, mate_line), device_id_type=MESH,
        )

    def deliver_copy(level):
        return pltpu.make_async_remote_copy(
            src_ref=own.at[level], dst_ref=out.at[rows_of(d), :],
            send_sem=grad_send.at[level], recv_sem=grad_recv.at[d],
            device_id=(level, line), device_id_type=MESH,
        )

    def deliver(level):
        swap(level).wait_recv()
        both = own[level].astype(F32) + got[level].astype(F32)

        @pl.when(level == d)
        def _():
            out[rows_of(d), :] = both.astype(BF16)

        @pl.when(level != d)
        def _():
            own[level] = both.astype(BF16)
            deliver_copy(level).start()

    for level in range(sections):
        if level > 0:
            @pl.when(level != d)
            def _():
                forward(level, theirs).wait_recv()
                turn(level, slice(0, order))

        if level + 1 < sections:
            @pl.when(level + 1 != d)
            def _():
                arrived_slow(level + 1).wait_recv()
                forward(level + 1, mine).start()

        if level > 0:
            deliver(level - 1)
        for stage in (rotate, solve_inline, solve_crossline):
            for slot in range(slots):
                stage(level, slot)
        own[level] = total[:, mine].astype(BF16)
        sent[level] = total[:, theirs].astype(BF16)
        swap(level).start()
    deliver(sections - 1)

    for copy in zone_copies + slow_copies:
        copy.wait_send()
    rec_copy.wait_send()
    for level in range(sections):
        forward(level, mine).wait_send()
        swap(level).wait_send()

        @pl.when(level != d)
        def _():
            deliver_copy(level).wait_send()
            pltpu.make_async_remote_copy(
                src_ref=own.at[level], dst_ref=out.at[rows_of(level), :],
                send_sem=grad_send.at[0], recv_sem=grad_recv.at[level],
                device_id=(level, line), device_id_type=MESH,
            ).wait_recv()


def per_device(
    receiver_data, source_amp, source_x, source_y, omegas, slowness, inverses, zones_x, zones_y
):
    sections = lax.axis_size("depth")
    freqs, _, width_x, width_y = receiver_data.shape
    order = inverses.shape[-1]
    pair = order // width_y
    points = source_x.shape[0]
    zone_count = inverses.shape[1]
    slots = freqs // pair
    assert pair == 2 and width_x == order * sections and slowness.shape[0] == 1
    vmem = pl.BlockSpec(memory_space=pltpu.VMEM)
    smem = pl.BlockSpec(memory_space=pltpu.SMEM)
    anywhere = pl.BlockSpec(memory_space=pl.ANY)
    dma = pltpu.SemaphoreType.DMA
    out = pl.pallas_call(
        functools.partial(kernel, sections, pair, 32),
        out_shape=pltpu.VMEM((width_x, width_y), BF16),
        in_specs=[anywhere, vmem, vmem, vmem, smem, anywhere, anywhere, vmem, vmem],
        out_specs=vmem,
        scratch_shapes=[
            pltpu.VMEM((sections, order, order), jnp.int16),
            pltpu.VMEM((width_x, width_y), F32),
            pltpu.VMEM((width_x, width_y), jnp.int16),
            pltpu.VMEM((slots, 2, order, order), BF16),
            pltpu.VMEM((slots, 2, 2, order, order), BF16),
            pltpu.VMEM((slots, zone_count, 2, order, order), BF16),
            pltpu.VMEM((8, 128), jnp.int32),
            pltpu.VMEM((sections, 8, 128), jnp.int32),
            pltpu.SMEM((sections, 8, 128), jnp.int32),
            pltpu.VMEM((sections, slots, 2, order, order), F32),
            pltpu.VMEM((slots, 2 * order, 2 * order), BF16),
            pltpu.VMEM((slots, 2 * order, 2 * order), BF16),
            pltpu.VMEM((sections, order, width_y), BF16),
            pltpu.VMEM((sections, order, width_y), BF16),
            pltpu.VMEM((sections, order, width_y), BF16),
            pltpu.VMEM((order, order), F32),
            dma((4,)),
            dma((sections,)), dma((sections,)),
            dma((sections,)), dma((sections,)),
            dma((sections,)), dma((sections,)),
            dma, dma,
            dma((sections,)), dma((sections,)),
            dma((sections,)), dma((sections,)),
        ],
        compiler_params=pltpu.CompilerParams(collective_id=0, has_side_effects=True),
    )(
        receiver_data, source_amp, source_x.reshape(1, points), source_y.reshape(1, points),
        omegas, slowness, inverses, zones_x, zones_y,
    )
    return out.astype(F32)[None]


def solution(mesh):
    in_specs = (
        P(None, None, None, "xline"),
        P(),
        P(),
        P(),
        P(),
        P("depth", None, "xline"),
        P(),
        P("depth", None),
        P("depth", None),
    )
    out_specs = P("depth", None, "xline")
    return jax.shard_map(
        per_device, mesh=mesh, in_specs=in_specs, out_specs=out_specs, check_vma=False
    )
```

profile of v0, /device:TPU:23, one launch (start us, length us, event | category | flops | bytes accessed | tf_op | source)
XLA Modules:
  0.0 22.8 jit_solution(7682069045666603640)
XLA Ops:
  0.0 21.9 %shard_map.91 = bf16[1024,128]{1,0:T(8,128)(2,1)S(1)} custom-call(bf16[4,2,1024,128]{3,2,1,0:T(8,128)(2,1)} %recv_in.1, bf16[4,2,256]{2,1,0:T(2,128)(2,1)} %amp.1, s32[1,256]{1,0:T(1,128)} %bitcast.5, s32[1,256]{1,0:T(1,128)} %bitcast.6, f32[4]{0:T(128)} %omegas.1, f32[1,1024,128]{2,1,0:T(8,128)} %slow_in.1, bf16[4,4,2,256,256]{4,3,2,1,0:T(8,128)(2,1)} %table_in.1, ...), custom_call_target="tpu_custom_call" | custom-call | tf_op jit(solution)/shard_map/pallas_call | solution.py:324
  22.0 0.8 %bitcast_convert_fusion = f32[1,1024,128]{2,1,0:T(8,128)} fusion(bf16[1024,128]{1,0:T(8,128)(2,1)S(1)} %shard_map.91), kind=kLoop, calls=%fused_computation | loop fusion | flops 131072 | bytes 786432 | tf_op jit(solution)/shard_map/broadcast_in_dim | solution.py:359
where the time goes:
time: 22.9 us; the launch traced here: 22.8 us
  Pallas kernels  21.9 us (96%)
  other arithmetic  0.83 us (4%)
    pallas_call x1, Pallas kernels, per_device(): pl.pallas_call(functools.partial(kernel, sections, pair, 32), out_shape=p...  21.9 us
    broadcast_in_dim x1, other arithmetic, per_device(): return out.astype(F32)[None]  0.83 us

commit v1 on v0

v1 whole, which is shorter than its diff:
```python
import functools
import math

import jax
import jax.numpy as jnp
import numpy as np
from jax import lax
from jax.experimental import pallas as pl
from jax.experimental.pallas import tpu as pltpu
from jax.sharding import PartitionSpec as P

MESH = pl.DeviceIdType.MESH
F32 = jnp.float32
BF16 = jnp.bfloat16

SLOW_LOW, SLOW_HIGH = 0.2, 2.0
OMEGA_LOW, OMEGA_HIGH = 0.5, 3.0
SLOW_MID = 0.5 * (SLOW_LOW + SLOW_HIGH)
CODE_STEP = (SLOW_HIGH - SLOW_LOW) / 65532.0
HALF_SPAN = 0.5 * max(OMEGA_HIGH * SLOW_HIGH - math.pi, math.pi - OMEGA_LOW * SLOW_LOW) + 0.01


def fitted(function, count):
    nodes = np.cos(np.pi * (np.arange(64) + 0.5) / 64)
    square = 0.5 * HALF_SPAN**2 * (nodes + 1.0)
    fit = np.polynomial.Chebyshev.fit(square, function(np.sqrt(square)), count - 1)
    return [float(term) for term in fit.convert(kind=np.polynomial.Polynomial).coef]


PARTS = 2
ROOT2 = math.sqrt(2.0)
SIN_TERMS = fitted(lambda t: ROOT2 * np.sin(t) / t, 5)
COS_TERMS = fitted(lambda t: -ROOT2 * np.cos(t), 5)


def series(square, terms):
    total = square * terms[-1] + terms[-2]
    for term in terms[-3::-1]:
        total = total * square + term
    return total


def sincos(half):
    square = half * half
    root_sine = series(square, SIN_TERMS) * half
    return root_sine * series(square, COS_TERMS), root_sine * root_sine - 1.0


def block_form(blocks):
    k_real, k_imag = blocks[0], blocks[1]
    top = jnp.concatenate([k_real, -k_imag], axis=1)
    bottom = jnp.concatenate([k_imag, k_real], axis=1)
    return jnp.concatenate([top, bottom], axis=0)


def kernel(
    sections, pair, rows, recv_in, amp_in, src_x_in, src_y_in, omegas_in, slow_in, table_in,
    zones_x_in, zones_y_in,
    out, slow, slow_raw, code, rec, wave, table, amp, src_x, src_y, omegas, zones_x, zones_y,
    zones, zone_buf, zone_rows, trig, rotated, inline, grad, got, total,
    load_sems, local_sems, zone_sems, zone_send, zone_recv, slow_send, slow_recv, fwd_send, fwd_recv,
    rec_send, rec_recv, swap_send, swap_recv, last_send, last_recv, grad_send, grad_recv, tail_send,
    tail_recv, ready,
):
    d = lax.axis_index("depth")
    line = lax.axis_index("xline")
    q = lax.rem(line, pair)
    block = line // pair
    mate_line = line + 1 - 2 * q
    width = recv_in.shape[3]
    order = pair * width
    slots = wave.shape[0]
    last = sections - 1
    parts = last_send.shape[0]
    mine = pl.ds(pl.multiple_of(q * width, width), width)
    theirs = pl.ds(pl.multiple_of((1 - q) * width, width), width)

    def rows_of(section):
        return pl.ds(pl.multiple_of(section * order, order), order)

    near = d + 1 - 2 * lax.rem(d, 2)
    next_to = d + 2 - 4 * (d // 2)
    far = last - d
    others = [far, near, next_to]
    FAR, NEAR, NEXT = range(3)

    barrier = pltpu.get_barrier_semaphore()
    for device in ((near, line), (next_to, line), (d, mate_line)):
        pl.semaphore_signal(barrier, inc=1, device_id=device, device_id_type=MESH)

    freqs = pl.ds(q * slots, slots)
    loads = [
        pltpu.make_async_copy(
            slow_in.at[0, rows_of(section), :], slow_raw.at[rows_of(section), :], load_sems.at[k]
        )
        for k, section in enumerate(others + [d])
    ]
    small = [
        pltpu.make_async_copy(source, target, local_sems.at[k])
        for k, (source, target) in enumerate((
            (zones_x_in, zones_x), (zones_y_in, zones_y), (omegas_in, omegas),
            (amp_in, amp), (src_x_in, src_x), (src_y_in, src_y),
        ))
    ]
    rec_load = pltpu.make_async_copy(
        recv_in.at[freqs, :, rows_of(d), :], rec.at[:, :, :, mine], local_sems.at[len(small)]
    )
    table_load = pltpu.make_async_copy(
        table_in.at[freqs], table, local_sems.at[len(small) + 1]
    )
    for copy in loads + small + [rec_load]:
        copy.start()

    def encode(section):
        part = rows_of(section)
        scaled = (slow_raw[part, :] - SLOW_MID) * (1.0 / CODE_STEP)
        return jnp.round(scaled).astype(jnp.int32).astype(jnp.int16)

    zones[...] = jnp.zeros_like(zones)
    small[0].wait()
    small[1].wait()
    zones[0:1, 0:zones_x.shape[1]] = zones_x[...]
    zones[1:2, 0:zones_y.shape[1]] = zones_y[...]
    zone_buf[d] = zones[...]
    for k, section in enumerate(others):
        loads[k].wait()
        code[rows_of(section), :] = encode(section)
    loads[len(others)].wait()
    slow[d, :, mine] = encode(d)
    table_load.start()

    zone_copies, slow_copies = [], []
    for k, other in enumerate(others):
        zone_copies.append(
            pltpu.make_async_remote_copy(
                src_ref=zones, dst_ref=zone_buf.at[d], send_sem=zone_send.at[k],
                recv_sem=zone_recv.at[d], device_id=(other, line), device_id_type=MESH,
            )
        )
        slow_copies.append(
            pltpu.make_async_remote_copy(
                src_ref=code.at[rows_of(other), :], dst_ref=slow.at[d, :, mine],
                send_sem=slow_send.at[k], recv_sem=slow_recv.at[d],
                device_id=(other, line), device_id_type=MESH,
            )
        )
    rec_copy = pltpu.make_async_remote_copy(
        src_ref=recv_in.at[pl.ds((1 - q) * slots, slots), :, rows_of(d), :],
        dst_ref=rec.at[:, :, :, mine], send_sem=rec_send, recv_sem=rec_recv,
        device_id=(d, mate_line), device_id_type=MESH,
    )

    def share(k):
        zone_copies[k].start()
        slow_copies[k].start()

    def arrived(level):
        zone = pltpu.make_async_remote_copy(
            src_ref=zones, dst_ref=zone_buf.at[level], send_sem=zone_send.at[0],
            recv_sem=zone_recv.at[level], device_id=(d, mate_line), device_id_type=MESH,
        )
        rest = pltpu.make_async_remote_copy(
            src_ref=slow.at[level, :, mine], dst_ref=slow.at[level, :, mine],
            send_sem=slow_send.at[0], recv_sem=slow_recv.at[level],
            device_id=(d, mate_line), device_id_type=MESH,
        )
        return zone, rest

    def forward(level, half):
        return pltpu.make_async_remote_copy(
            src_ref=slow.at[level, :, half], dst_ref=slow.at[level, :, half],
            send_sem=fwd_send.at[level], recv_sem=fwd_recv.at[level],
            device_id=(d, mate_line), device_id_type=MESH,
        )

    def zone_copy(level):
        return pltpu.make_async_copy(
            zone_buf.at[level], zone_rows.at[level], zone_sems.at[level]
        )

    def receive(level):
        @pl.when(level != d)
        def _():
            for copy in arrived(level):
                copy.wait_recv()
        zone_copy(level).start()
        forward(level, mine).start()

    pl.semaphore_wait(barrier, pair + 1)
    pl.semaphore_signal(ready, inc=1, device_id=(near, line), device_id_type=MESH)

    @pl.when(d == 0)
    def _():
        share(NEAR)
        share(NEXT)

    @pl.when(d != 0)
    def _():
        pl.semaphore_wait(ready, 1)
        share(FAR)
        share(NEAR)
        share(NEXT)

    rec_copy.start()
    for copy in small[2:]:
        copy.wait()

    points = src_x.shape[1]
    cells = lax.broadcasted_iota(jnp.int32, (order, points), 0)
    hit_x = cells + d * order == src_x[...]
    hit_y = jnp.where(cells + block * order == src_y[...], 1.0, 0.0).astype(BF16)
    for slot in range(slots):
        for part in range(2):
            amps = amp[q * slots + slot, pl.ds(part, 1), :].astype(F32)
            spread = jnp.where(hit_x, amps, 0.0).astype(BF16)
            field = lax.dot_general(
                spread, hit_y, (((1,), (1,)), ((), ())), preferred_element_type=F32
            )
            wave[slot, 0, part] = field.astype(BF16)

    @pl.when(d == 0)
    def _():
        pl.semaphore_wait(ready, 1)
        share(FAR)

    def turn(level, slot, lanes):
        omega = omegas[q * slots + slot]
        slope = omega * (0.5 * CODE_STEP)
        shift = omega * (0.5 * SLOW_MID) - 0.5 * math.pi
        for start in range(0, order, rows):
            part = slice(start, start + rows)
            value = slow[level, part, lanes].astype(jnp.int32).astype(F32)
            sine, cosine = sincos(value * slope + shift)
            trig[slot, 0, part, lanes] = sine
            trig[slot, 1, part, lanes] = cosine

    def rotate(slot):
        for start in range(0, order, rows):
            part = slice(start, start + rows)
            sine, cosine = trig[slot, 0, part, :], trig[slot, 1, part, :]
            for field in range(2):
                real = wave[slot, field, 0, part, :].astype(F32)
                imag = wave[slot, field, 1, part, :].astype(F32)
                lanes = slice(field * order, (field + 1) * order)
                rotated[slot, part, lanes] = (real * cosine - imag * sine).astype(BF16)
                rotated[slot, order + start:order + start + rows, lanes] = (
                    real * sine + imag * cosine
                ).astype(BF16)

    def solve_inline(level, slot):
        m_x = block_form(table[slot, zone_rows[level, 0, d]])
        for field in range(2):
            lanes = slice(field * order, (field + 1) * order)
            value = rotated[slot, :, lanes]
            solved = value.astype(F32) + jnp.dot(m_x, value, preferred_element_type=F32)
            solved = solved.astype(BF16)
            inline[slot, lanes, 0:order] = solved[:order]
            inline[slot, lanes, order:] = solved[order:]

    def solve_crossline(level, slot, part):
        omega = omegas[q * slots + slot]
        m_y = block_form(table[slot, zone_rows[level, 1, block]])
        count = part.stop - part.start
        value = jnp.concatenate(
            [inline[slot, part, :], inline[slot, order + part.start:order + part.stop, :]], axis=0
        )
        product = []
        for half in range(2):
            lanes = slice(half * order, (half + 1) * order)
            solved = value[:, lanes].astype(F32) + lax.dot_general(
                value, m_y[lanes], (((1,), (1,)), ((), ())), preferred_element_type=F32
            )
            product.append(solved[:count] * solved[count:])
            if level < last:
                wave[slot, 0, half, part] = solved[:count].astype(BF16)
                wave[slot, 1, half, part] = solved[count:].astype(BF16)
        image = (omega * omega) * (product[0] - product[1])
        if slot > 0:
            image = total[part, :] + image
        if slot + 1 < slots:
            total[part, :] = image
        else:
            grad[level, part, :] = image.astype(BF16)

    def swap(level):
        return pltpu.make_async_remote_copy(
            src_ref=grad.at[level, :, theirs], dst_ref=got.at[level],
            send_sem=swap_send.at[level], recv_sem=swap_recv.at[level],
            device_id=(d, mate_line), device_id_type=MESH,
        )

    def swap_part(k):
        part = pl.ds(k * (order // parts), order // parts)
        return pltpu.make_async_remote_copy(
            src_ref=grad.at[last, part, theirs], dst_ref=got.at[last, part],
            send_sem=last_send.at[k], recv_sem=last_recv.at[k],
            device_id=(d, mate_line), device_id_type=MESH,
        )

    def deliver_copy(level):
        return pltpu.make_async_remote_copy(
            src_ref=got.at[level], dst_ref=out.at[rows_of(d), :],
            send_sem=grad_send.at[level], recv_sem=grad_recv.at[d],
            device_id=(level, line), device_id_type=MESH,
        )

    def section_part(section, k):
        count = order // parts
        return pl.ds(pl.multiple_of(section * order + k * count, count), count)

    def deliver_part(k, section):
        part = pl.ds(k * (order // parts), order // parts)
        return pltpu.make_async_remote_copy(
            src_ref=got.at[last, part], dst_ref=out.at[section_part(section, k), :],
            send_sem=tail_send.at[k], recv_sem=tail_recv.at[section, k],
            device_id=(last, line), device_id_type=MESH,
        )

    def deliver(level):
        swap(level).wait_recv()
        both = grad[level, :, mine].astype(F32) + got[level].astype(F32)

        @pl.when(level == d)
        def _():
            out[rows_of(d), :] = both.astype(BF16)

        @pl.when(level != d)
        def _():
            got[level] = both.astype(BF16)
            deliver_copy(level).start()

    def deliver_last(k):
        part = pl.ds(k * (order // parts), order // parts)
        swap_part(k).wait_recv()
        both = grad[last, part, mine].astype(F32) + got[last, part].astype(F32)

        @pl.when(d == last)
        def _():
            out[section_part(d, k), :] = both.astype(BF16)

        @pl.when(d != last)
        def _():
            got[last, part] = both.astype(BF16)
            deliver_part(k, d).start()

    whole = slice(0, order)
    rec_load.wait()
    rec_copy.wait_recv()
    for slot in range(slots):
        wave[slot, 1, 0] = rec[slot, 0]
        wave[slot, 1, 1] = -rec[slot, 1]
    table_load.wait()

    receive(0)
    for slot in range(slots):
        turn(0, slot, mine)
    if sections > 1:
        receive(1)
    zone_copy(0).wait()
    forward(0, theirs).wait_recv()
    for slot in range(slots):
        turn(0, slot, theirs)
    for slot in range(slots):
        rotate(slot)
        solve_inline(0, slot)

    for level in range(1, sections):
        if level + 1 < sections:
            receive(level + 1)
        if level > 1:
            swap(level - 2).start()
        if level > 2:
            deliver(level - 3)
        zone_copy(level).wait()
        forward(level, theirs).wait_recv()
        for slot in range(slots):
            solve_crossline(level - 1, slot, whole)
            turn(level, slot, whole)
        for slot in range(slots):
            rotate(slot)
            solve_inline(level, slot)
    swap(last - 1).start()
    for k in range(parts):
        part = slice(k * (order // parts), (k + 1) * (order // parts))
        for slot in range(slots):
            solve_crossline(last, slot, part)
        swap_part(k).start()
        if k == 0:
            for level in range(max(last - 2, 0), last):
                deliver(level)
    for k in range(parts):
        deliver_last(k)

    for copy in zone_copies + slow_copies:
        copy.wait_send()
    rec_copy.wait_send()
    for level in range(sections):
        forward(level, mine).wait_send()
    for level in range(last):
        swap(level).wait_send()

        @pl.when(level != d)
        def _():
            deliver_copy(level).wait_send()
    for k in range(parts):
        swap_part(k).wait_send()

    @pl.when(d != last)
    def _():
        for k in range(parts):
            deliver_part(k, d).wait_send()
        for other in others:
            pltpu.make_async_remote_copy(
                src_ref=got.at[0], dst_ref=out.at[rows_of(other), :],
                send_sem=grad_send.at[0], recv_sem=grad_recv.at[other],
                device_id=(d, mate_line), device_id_type=MESH,
            ).wait_recv()

    @pl.when(d == last)
    def _():
        for other in others:
            for k in range(parts):
                deliver_part(k, other).wait_recv()


def per_device(
    receiver_data, source_amp, source_x, source_y, omegas, slowness, inverses, zones_x, zones_y
):
    sections = lax.axis_size("depth")
    freqs, _, width_x, width_y = receiver_data.shape
    order = inverses.shape[-1]
    pair = order // width_y
    points = source_x.shape[0]
    zone_count = inverses.shape[1]
    slots = freqs // pair
    assert pair == 2 and sections == 4 and width_x == order * sections and slowness.shape[0] == 1
    vmem = pl.BlockSpec(memory_space=pltpu.VMEM)
    anywhere = pl.BlockSpec(memory_space=pl.ANY)
    dma = pltpu.SemaphoreType.DMA
    out = pl.pallas_call(
        functools.partial(kernel, sections, pair, 32),
        out_shape=pltpu.VMEM((width_x, width_y), BF16),
        in_specs=[anywhere] * 9,
        out_specs=vmem,
        scratch_shapes=[
            pltpu.VMEM((sections, order, order), jnp.int16),
            pltpu.VMEM((width_x, width_y), F32),
            pltpu.VMEM((width_x, width_y), jnp.int16),
            pltpu.VMEM((slots, 2, order, order), BF16),
            pltpu.VMEM((slots, 2, 2, order, order), BF16),
            pltpu.VMEM((slots, zone_count, 2, order, order), BF16),
            pltpu.VMEM(source_amp.shape, BF16),
            pltpu.VMEM((1, points), jnp.int32),
            pltpu.VMEM((1, points), jnp.int32),
            pltpu.SMEM(omegas.shape, F32),
            pltpu.VMEM(zones_x.shape, jnp.int32),
            pltpu.VMEM(zones_y.shape, jnp.int32),
            pltpu.VMEM((8, 128), jnp.int32),
            pltpu.VMEM((sections, 8, 128), jnp.int32),
            pltpu.SMEM((sections, 8, 128), jnp.int32),
            pltpu.VMEM((slots, 2, order, order), F32),
            pltpu.VMEM((slots, 2 * order, 2 * order), BF16),
            pltpu.VMEM((slots, 2 * order, 2 * order), BF16),
            pltpu.VMEM((sections, order, order), BF16),
            pltpu.VMEM((sections, order, width_y), BF16),
            pltpu.VMEM((order, order), F32),
            dma((sections,)), dma((8,)), dma((sections,)),
            dma((sections,)), dma((sections,)),
            dma((sections,)), dma((sections,)),
            dma((sections,)), dma((sections,)),
            dma, dma,
            dma((sections,)), dma((sections,)),
            dma((PARTS,)), dma((PARTS,)),
            dma((sections,)), dma((sections,)),
            dma((PARTS,)), dma((sections, PARTS)),
            pltpu.SemaphoreType.REGULAR,
        ],
        compiler_params=pltpu.CompilerParams(collective_id=0, has_side_effects=True),
    )(
        receiver_data, source_amp, source_x.reshape(1, points), source_y.reshape(1, points),
        omegas, slowness, inverses, zones_x, zones_y,
    )
    return out.astype(F32)[None]


def solution(mesh):
    in_specs = (
        P(None, None, None, "xline"),
        P(),
        P(),
        P(),
        P(),
        P("depth", None, "xline"),
        P(),
        P("depth", None),
        P("depth", None),
    )
    out_specs = P("depth", None, "xline")
    return jax.shard_map(
        per_device, mesh=mesh, in_specs=in_specs, out_specs=out_specs, check_vma=False
    )
```

time: 22.9 us -> 21.4 us (0.934)
  the two profiles are of different devices: /device:TPU:23 before, /device:TPU:0 now
where the time goes in v1:
time: 21.4 us; the launch traced here: 21.3 us
  Pallas kernels  20.4 us (95%)
  other arithmetic  0.83 us (4%)
    pallas_call x1, Pallas kernels, per_device(): pl.pallas_call(functools.partial(kernel, sections, pair, 32), out_shape=p...  20.4 us
    broadcast_in_dim x1, other arithmetic, per_device(): return out.astype(F32)[None]  0.83 us

profile of v1, /device:TPU:0, one launch (start us, length us, event | category | flops | bytes accessed | tf_op | source)
XLA Modules:
  0.0 21.3 jit_solution(2744299024646108718)
XLA Ops:
  0.0 20.4 %shard_map.91 = bf16[1024,128]{1,0:T(8,128)(2,1)S(1)} custom-call(bf16[4,2,1024,128]{3,2,1,0:T(8,128)(2,1)} %recv_in.1, bf16[4,2,256]{2,1,0:T(2,128)(2,1)} %amp_in.1, s32[1,256]{1,0:T(1,128)} %bitcast.5, s32[1,256]{1,0:T(1,128)} %bitcast.6, f32[4]{0:T(128)} %omegas_in.1, f32[1,1024,128]{2,1,0:T(8,128)} %slow_in.1, bf16[4,4,2,256,256]{4,3,2,1,0:T(8,128)(2,1)} %table_in.1, ...), custom_call_target="tpu_custom_call" | custom-call | tf_op jit(solution)/shard_map/pallas_call | solution.py:440
  20.4 0.8 %bitcast_convert_fusion = f32[1,1024,128]{2,1,0:T(8,128)} fusion(bf16[1024,128]{1,0:T(8,128)(2,1)S(1)} %shard_map.91), kind=kLoop, calls=%fused_computation | loop fusion | flops 131072 | bytes 786432 | tf_op jit(solution)/shard_map/broadcast_in_dim | solution.py:483

commit v2 on v1

--- a/solution.py
+++ b/solution.py
@@ -29,7 +29,7 @@
 
 PARTS = 2
 ROOT2 = math.sqrt(2.0)
-SIN_TERMS = fitted(lambda t: ROOT2 * np.sin(t) / t, 5)
+SIN_TERMS = fitted(lambda t: ROOT2 * np.sin(t) / t, 4)
 COS_TERMS = fitted(lambda t: -ROOT2 * np.cos(t), 5)
 
 
@@ -46,17 +46,10 @@
     return root_sine * series(square, COS_TERMS), root_sine * root_sine - 1.0
 
 
-def block_form(blocks):
-    k_real, k_imag = blocks[0], blocks[1]
-    top = jnp.concatenate([k_real, -k_imag], axis=1)
-    bottom = jnp.concatenate([k_imag, k_real], axis=1)
-    return jnp.concatenate([top, bottom], axis=0)
-
-
 def kernel(
     sections, pair, rows, recv_in, amp_in, src_x_in, src_y_in, omegas_in, slow_in, table_in,
     zones_x_in, zones_y_in,
-    out, slow, slow_raw, code, rec, wave, table, amp, src_x, src_y, omegas, zones_x, zones_y,
+    out, slow, slow_raw, code, rec, wave, table, forms, amp, src_x, src_y, omegas, zones_x, zones_y,
     zones, zone_buf, zone_rows, trig, rotated, inline, grad, got, total,
     load_sems, local_sems, zone_sems, zone_send, zone_recv, slow_send, slow_recv, fwd_send, fwd_recv,
     rec_send, rec_recv, swap_send, swap_recv, last_send, last_recv, grad_send, grad_recv, tail_send,
@@ -189,18 +182,8 @@
     pl.semaphore_wait(barrier, pair + 1)
     pl.semaphore_signal(ready, inc=1, device_id=(near, line), device_id_type=MESH)
 
-    @pl.when(d == 0)
-    def _():
-        share(NEAR)
-        share(NEXT)
-
-    @pl.when(d != 0)
-    def _():
-        pl.semaphore_wait(ready, 1)
-        share(FAR)
-        share(NEAR)
-        share(NEXT)
-
+    share(NEAR)
+    share(NEXT)
     rec_copy.start()
     for copy in small[2:]:
         copy.wait()
@@ -218,48 +201,55 @@
             )
             wave[slot, 0, part] = field.astype(BF16)
 
-    @pl.when(d == 0)
-    def _():
-        pl.semaphore_wait(ready, 1)
-        share(FAR)
-
-    def turn(level, slot, lanes):
-        omega = omegas[q * slots + slot]
-        slope = omega * (0.5 * CODE_STEP)
-        shift = omega * (0.5 * SLOW_MID) - 0.5 * math.pi
+    pl.semaphore_wait(ready, 1)
+    share(FAR)
+
+    table_load.wait()
+    for slot in range(slots):
+        for zone in range(table.shape[1]):
+            k_real, k_imag = table[slot, zone, 0], table[slot, zone, 1]
+            forms[slot, zone, :order, :order] = k_real
+            forms[slot, zone, :order, order:] = -k_imag
+            forms[slot, zone, order:, :order] = k_imag
+            forms[slot, zone, order:, order:] = k_real
+
+    def turn(level, lanes):
         for start in range(0, order, rows):
             part = slice(start, start + rows)
             value = slow[level, part, lanes].astype(jnp.int32).astype(F32)
-            sine, cosine = sincos(value * slope + shift)
-            trig[slot, 0, part, lanes] = sine
-            trig[slot, 1, part, lanes] = cosine
+            for slot in range(slots):
+                omega = omegas[q * slots + slot]
+                slope = omega * (0.5 * CODE_STEP)
+                shift = omega * (0.5 * SLOW_MID) - 0.5 * math.pi
+                sine, cosine = sincos(value * slope + shift)
+                trig[slot, 0, part, lanes] = sine.astype(BF16)
+                trig[slot, 1, part, lanes] = cosine.astype(BF16)
 
     def rotate(slot):
         for start in range(0, order, rows):
             part = slice(start, start + rows)
             sine, cosine = trig[slot, 0, part, :], trig[slot, 1, part, :]
             for field in range(2):
-                real = wave[slot, field, 0, part, :].astype(F32)
-                imag = wave[slot, field, 1, part, :].astype(F32)
+                real, imag = wave[slot, field, 0, part, :], wave[slot, field, 1, part, :]
                 lanes = slice(field * order, (field + 1) * order)
-                rotated[slot, part, lanes] = (real * cosine - imag * sine).astype(BF16)
+                rotated[slot, part, lanes] = real * cosine - imag * sine
                 rotated[slot, order + start:order + start + rows, lanes] = (
                     real * sine + imag * cosine
-                ).astype(BF16)
+                )
 
     def solve_inline(level, slot):
-        m_x = block_form(table[slot, zone_rows[level, 0, d]])
+        m_x = forms[slot, zone_rows[level, 0, d]]
         for field in range(2):
             lanes = slice(field * order, (field + 1) * order)
             value = rotated[slot, :, lanes]
-            solved = value.astype(F32) + jnp.dot(m_x, value, preferred_element_type=F32)
-            solved = solved.astype(BF16)
+            added = jnp.dot(m_x, value, preferred_element_type=F32).astype(BF16)
+            solved = value + added
             inline[slot, lanes, 0:order] = solved[:order]
             inline[slot, lanes, order:] = solved[order:]
 
     def solve_crossline(level, slot, part):
         omega = omegas[q * slots + slot]
-        m_y = block_form(table[slot, zone_rows[level, 1, block]])
+        m_y = forms[slot, zone_rows[level, 1, block]]
         count = part.stop - part.start
         value = jnp.concatenate(
             [inline[slot, part, :], inline[slot, order + part.start:order + part.stop, :]], axis=0
@@ -267,13 +257,14 @@
         product = []
         for half in range(2):
             lanes = slice(half * order, (half + 1) * order)
-            solved = value[:, lanes].astype(F32) + lax.dot_general(
+            added = lax.dot_general(
                 value, m_y[lanes], (((1,), (1,)), ((), ())), preferred_element_type=F32
             )
-            product.append(solved[:count] * solved[count:])
+            solved = value[:, lanes] + added.astype(BF16)
+            product.append(solved[:count].astype(F32) * solved[count:].astype(F32))
             if level < last:
-                wave[slot, 0, half, part] = solved[:count].astype(BF16)
-                wave[slot, 1, half, part] = solved[count:].astype(BF16)
+                wave[slot, 0, half, part] = solved[:count]
+                wave[slot, 1, half, part] = solved[count:]
         image = (omega * omega) * (product[0] - product[1])
         if slot > 0:
             image = total[part, :] + image
@@ -349,17 +340,13 @@
     for slot in range(slots):
         wave[slot, 1, 0] = rec[slot, 0]
         wave[slot, 1, 1] = -rec[slot, 1]
-    table_load.wait()
-
     receive(0)
-    for slot in range(slots):
-        turn(0, slot, mine)
+    turn(0, mine)
     if sections > 1:
         receive(1)
     zone_copy(0).wait()
     forward(0, theirs).wait_recv()
-    for slot in range(slots):
-        turn(0, slot, theirs)
+    turn(0, theirs)
     for slot in range(slots):
         rotate(slot)
         solve_inline(0, slot)
@@ -375,7 +362,7 @@
         forward(level, theirs).wait_recv()
         for slot in range(slots):
             solve_crossline(level - 1, slot, whole)
-            turn(level, slot, whole)
+        turn(level, whole)
         for slot in range(slots):
             rotate(slot)
             solve_inline(level, slot)
@@ -449,6 +436,7 @@
             pltpu.VMEM((slots, 2, order, order), BF16),
             pltpu.VMEM((slots, 2, 2, order, order), BF16),
             pltpu.VMEM((slots, zone_count, 2, order, order), BF16),
+            pltpu.VMEM((slots, zone_count, 2 * order, 2 * order), BF16),
             pltpu.VMEM(source_amp.shape, BF16),
             pltpu.VMEM((1, points), jnp.int32),
             pltpu.VMEM((1, points), jnp.int32),
@@ -458,7 +446,7 @@
             pltpu.VMEM((8, 128), jnp.int32),
             pltpu.VMEM((sections, 8, 128), jnp.int32),
             pltpu.SMEM((sections, 8, 128), jnp.int32),
-            pltpu.VMEM((slots, 2, order, order), F32),
+            pltpu.VMEM((slots, 2, order, order), BF16),
             pltpu.VMEM((slots, 2 * order, 2 * order), BF16),
             pltpu.VMEM((slots, 2 * order, 2 * order), BF16),
             pltpu.VMEM((sections, order, order), BF16),

time: 21.4 us -> 20 us (0.935)
  the two profiles are of different devices: /device:TPU:0 before, /device:TPU:19 now
where the time goes in v2:
time: 20 us; the launch traced here: 19.9 us
  Pallas kernels  19 us (95%)
  other arithmetic  0.83 us (4%)
    pallas_call x1, Pallas kernels, per_device(): pl.pallas_call(functools.partial(kernel, sections, pair, 32), out_shape=p...  19 us
    broadcast_in_dim x1, other arithmetic, per_device(): return out.astype(F32)[None]  0.83 us

profile of v2, /device:TPU:19, one launch (start us, length us, event | category | flops | bytes accessed | tf_op | source)
XLA Modules:
  0.0 19.9 jit_solution(12241029678081932726)
XLA Ops:
  0.0 19.0 %shard_map.91 = bf16[1024,128]{1,0:T(8,128)(2,1)S(1)} custom-call(bf16[4,2,1024,128]{3,2,1,0:T(8,128)(2,1)} %recv_in.1, bf16[4,2,256]{2,1,0:T(2,128)(2,1)} %amp_in.1, s32[1,256]{1,0:T(1,128)} %bitcast.5, s32[1,256]{1,0:T(1,128)} %bitcast.6, f32[4]{0:T(128)} %omegas_in.1, f32[1,1024,128]{2,1,0:T(8,128)} %slow_in.1, bf16[4,4,2,256,256]{4,3,2,1,0:T(8,128)(2,1)} %table_in.1, ...), custom_call_target="tpu_custom_call" | custom-call | tf_op jit(solution)/shard_map/pallas_call | solution.py:427
  19.1 0.8 %bitcast_convert_fusion = f32[1,1024,128]{2,1,0:T(8,128)} fusion(bf16[1024,128]{1,0:T(8,128)(2,1)S(1)} %shard_map.91), kind=kLoop, calls=%fused_computation | loop fusion | flops 131072 | bytes 786432 | tf_op jit(solution)/shard_map/broadcast_in_dim | solution.py:471

commit v3 on v2

--- a/solution.py
+++ b/solution.py
@@ -65,8 +65,6 @@
     slots = wave.shape[0]
     last = sections - 1
     parts = last_send.shape[0]
-    mine = pl.ds(pl.multiple_of(q * width, width), width)
-    theirs = pl.ds(pl.multiple_of((1 - q) * width, width), width)
 
     def rows_of(section):
         return pl.ds(pl.multiple_of(section * order, order), order)
@@ -96,7 +94,7 @@
         ))
     ]
     rec_load = pltpu.make_async_copy(
-        recv_in.at[freqs, :, rows_of(d), :], rec.at[:, :, :, mine], local_sems.at[len(small)]
+        recv_in.at[freqs, :, rows_of(d), :], rec.at[q], local_sems.at[len(small)]
     )
     table_load = pltpu.make_async_copy(
         table_in.at[freqs], table, local_sems.at[len(small) + 1]
@@ -119,7 +117,7 @@
         loads[k].wait()
         code[rows_of(section), :] = encode(section)
     loads[len(others)].wait()
-    slow[d, :, mine] = encode(d)
+    slow[d, q] = encode(d)
     table_load.start()
 
     zone_copies, slow_copies = [], []
@@ -132,14 +130,14 @@
         )
         slow_copies.append(
             pltpu.make_async_remote_copy(
-                src_ref=code.at[rows_of(other), :], dst_ref=slow.at[d, :, mine],
+                src_ref=code.at[rows_of(other), :], dst_ref=slow.at[d, q],
                 send_sem=slow_send.at[k], recv_sem=slow_recv.at[d],
                 device_id=(other, line), device_id_type=MESH,
             )
         )
     rec_copy = pltpu.make_async_remote_copy(
         src_ref=recv_in.at[pl.ds((1 - q) * slots, slots), :, rows_of(d), :],
-        dst_ref=rec.at[:, :, :, mine], send_sem=rec_send, recv_sem=rec_recv,
+        dst_ref=rec.at[q], send_sem=rec_send, recv_sem=rec_recv,
         device_id=(d, mate_line), device_id_type=MESH,
     )
 
@@ -153,7 +151,7 @@
             recv_sem=zone_recv.at[level], device_id=(d, mate_line), device_id_type=MESH,
         )
         rest = pltpu.make_async_remote_copy(
-            src_ref=slow.at[level, :, mine], dst_ref=slow.at[level, :, mine],
+            src_ref=slow.at[level, q], dst_ref=slow.at[level, q],
             send_sem=slow_send.at[0], recv_sem=slow_recv.at[level],
             device_id=(d, mate_line), device_id_type=MESH,
         )
@@ -161,7 +159,7 @@
 
     def forward(level, half):
         return pltpu.make_async_remote_copy(
-            src_ref=slow.at[level, :, half], dst_ref=slow.at[level, :, half],
+            src_ref=slow.at[level, half], dst_ref=slow.at[level, half],
             send_sem=fwd_send.at[level], recv_sem=fwd_recv.at[level],
             device_id=(d, mate_line), device_id_type=MESH,
         )
@@ -172,12 +170,17 @@
         )
 
     def receive(level):
+        zone, rest = arrived(level)
+
         @pl.when(level != d)
         def _():
-            for copy in arrived(level):
-                copy.wait_recv()
+            zone.wait_recv()
         zone_copy(level).start()
-        forward(level, mine).start()
+
+        @pl.when(level != d)
+        def _():
+            rest.wait_recv()
+        forward(level, q).start()
 
     pl.semaphore_wait(barrier, pair + 1)
     pl.semaphore_signal(ready, inc=1, device_id=(near, line), device_id_type=MESH)
@@ -213,29 +216,31 @@
             forms[slot, zone, order:, :order] = k_imag
             forms[slot, zone, order:, order:] = k_real
 
-    def turn(level, lanes):
+    def turn(level, half):
+        lanes = pl.ds(pl.multiple_of(half * width, width), width)
         for start in range(0, order, rows):
             part = slice(start, start + rows)
-            value = slow[level, part, lanes].astype(jnp.int32).astype(F32)
+            value = slow[level, half, part, :].astype(jnp.int32).astype(F32)
             for slot in range(slots):
                 omega = omegas[q * slots + slot]
                 slope = omega * (0.5 * CODE_STEP)
                 shift = omega * (0.5 * SLOW_MID) - 0.5 * math.pi
                 sine, cosine = sincos(value * slope + shift)
-                trig[slot, 0, part, lanes] = sine.astype(BF16)
-                trig[slot, 1, part, lanes] = cosine.astype(BF16)
+                trig[slot, 0, part, lanes] = sine
+                trig[slot, 1, part, lanes] = cosine
 
     def rotate(slot):
         for start in range(0, order, rows):
             part = slice(start, start + rows)
             sine, cosine = trig[slot, 0, part, :], trig[slot, 1, part, :]
             for field in range(2):
-                real, imag = wave[slot, field, 0, part, :], wave[slot, field, 1, part, :]
+                real = wave[slot, field, 0, part, :].astype(F32)
+                imag = wave[slot, field, 1, part, :].astype(F32)
                 lanes = slice(field * order, (field + 1) * order)
-                rotated[slot, part, lanes] = real * cosine - imag * sine
+                rotated[slot, part, lanes] = (real * cosine - imag * sine).astype(BF16)
                 rotated[slot, order + start:order + start + rows, lanes] = (
                     real * sine + imag * cosine
-                )
+                ).astype(BF16)
 
     def solve_inline(level, slot):
         m_x = forms[slot, zone_rows[level, 0, d]]
@@ -261,21 +266,24 @@
                 value, m_y[lanes], (((1,), (1,)), ((), ())), preferred_element_type=F32
             )
             solved = value[:, lanes] + added.astype(BF16)
-            product.append(solved[:count].astype(F32) * solved[count:].astype(F32))
+            product.append(solved[:count] * solved[count:])
             if level < last:
                 wave[slot, 0, half, part] = solved[:count]
                 wave[slot, 1, half, part] = solved[count:]
-        image = (omega * omega) * (product[0] - product[1])
+        image = (omega * omega) * (product[0] - product[1]).astype(F32)
         if slot > 0:
             image = total[part, :] + image
         if slot + 1 < slots:
             total[part, :] = image
         else:
-            grad[level, part, :] = image.astype(BF16)
+            for half in range(pair):
+                grad[level, half, part, :] = (
+                    image[:, half * width:(half + 1) * width].astype(BF16)
+                )
 
     def swap(level):
         return pltpu.make_async_remote_copy(
-            src_ref=grad.at[level, :, theirs], dst_ref=got.at[level],
+            src_ref=grad.at[level, 1 - q], dst_ref=got.at[level],
             send_sem=swap_send.at[level], recv_sem=swap_recv.at[level],
             device_id=(d, mate_line), device_id_type=MESH,
         )
@@ -283,7 +291,7 @@
     def swap_part(k):
         part = pl.ds(k * (order // parts), order // parts)
         return pltpu.make_async_remote_copy(
-            src_ref=grad.at[last, part, theirs], dst_ref=got.at[last, part],
+            src_ref=grad.at[last, 1 - q, part], dst_ref=got.at[last, part],
             send_sem=last_send.at[k], recv_sem=last_recv.at[k],
             device_id=(d, mate_line), device_id_type=MESH,
         )
@@ -309,7 +317,7 @@
 
     def deliver(level):
         swap(level).wait_recv()
-        both = grad[level, :, mine].astype(F32) + got[level].astype(F32)
+        both = grad[level, q].astype(F32) + got[level].astype(F32)
 
         @pl.when(level == d)
         def _():
@@ -323,7 +331,7 @@
     def deliver_last(k):
         part = pl.ds(k * (order // parts), order // parts)
         swap_part(k).wait_recv()
-        both = grad[last, part, mine].astype(F32) + got[last, part].astype(F32)
+        both = grad[last, q, part].astype(F32) + got[last, part].astype(F32)
 
         @pl.when(d == last)
         def _():
@@ -338,43 +346,40 @@
     rec_load.wait()
     rec_copy.wait_recv()
     for slot in range(slots):
-        wave[slot, 1, 0] = rec[slot, 0]
-        wave[slot, 1, 1] = -rec[slot, 1]
+        for half in range(pair):
+            lanes = slice(half * width, (half + 1) * width)
+            wave[slot, 1, 0, :, lanes] = rec[half, slot, 0]
+            wave[slot, 1, 1, :, lanes] = -rec[half, slot, 1]
     receive(0)
-    turn(0, mine)
-    if sections > 1:
-        receive(1)
+    turn(0, q)
+    receive(1)
     zone_copy(0).wait()
-    forward(0, theirs).wait_recv()
-    turn(0, theirs)
-    for slot in range(slots):
-        rotate(slot)
-        solve_inline(0, slot)
-
-    for level in range(1, sections):
-        if level + 1 < sections:
-            receive(level + 1)
-        if level > 1:
-            swap(level - 2).start()
-        if level > 2:
-            deliver(level - 3)
-        zone_copy(level).wait()
-        forward(level, theirs).wait_recv()
-        for slot in range(slots):
-            solve_crossline(level - 1, slot, whole)
-        turn(level, whole)
+    forward(0, 1 - q).wait_recv()
+    turn(0, 1 - q)
+    for level in range(sections):
         for slot in range(slots):
             rotate(slot)
             solve_inline(level, slot)
-    swap(last - 1).start()
+        if level == last:
+            break
+        if level + 2 < sections:
+            receive(level + 2)
+        if level > 0:
+            deliver(level - 1)
+        zone_copy(level + 1).wait()
+        forward(level + 1, 1 - q).wait_recv()
+        for slot in range(slots):
+            solve_crossline(level, slot, whole)
+        for half in range(pair):
+            turn(level + 1, half)
+        swap(level).start()
     for k in range(parts):
         part = slice(k * (order // parts), (k + 1) * (order // parts))
         for slot in range(slots):
             solve_crossline(last, slot, part)
         swap_part(k).start()
         if k == 0:
-            for level in range(max(last - 2, 0), last):
-                deliver(level)
+            deliver(last - 1)
     for k in range(parts):
         deliver_last(k)
 
@@ -382,7 +387,7 @@
         copy.wait_send()
     rec_copy.wait_send()
     for level in range(sections):
-        forward(level, mine).wait_send()
+        forward(level, q).wait_send()
     for level in range(last):
         swap(level).wait_send()
 
@@ -430,10 +435,10 @@
         in_specs=[anywhere] * 9,
         out_specs=vmem,
         scratch_shapes=[
-            pltpu.VMEM((sections, order, order), jnp.int16),
+            pltpu.VMEM((sections, pair, order, width_y), jnp.int16),
             pltpu.VMEM((width_x, width_y), F32),
             pltpu.VMEM((width_x, width_y), jnp.int16),
-            pltpu.VMEM((slots, 2, order, order), BF16),
+            pltpu.VMEM((pair, slots, 2, order, width_y), BF16),
             pltpu.VMEM((slots, 2, 2, order, order), BF16),
             pltpu.VMEM((slots, zone_count, 2, order, order), BF16),
             pltpu.VMEM((slots, zone_count, 2 * order, 2 * order), BF16),
@@ -446,10 +451,10 @@
             pltpu.VMEM((8, 128), jnp.int32),
             pltpu.VMEM((sections, 8, 128), jnp.int32),
             pltpu.SMEM((sections, 8, 128), jnp.int32),
-            pltpu.VMEM((slots, 2, order, order), BF16),
+            pltpu.VMEM((slots, 2, order, order), F32),
             pltpu.VMEM((slots, 2 * order, 2 * order), BF16),
             pltpu.VMEM((slots, 2 * order, 2 * order), BF16),
-            pltpu.VMEM((sections, order, order), BF16),
+            pltpu.VMEM((sections, pair, order, width_y), BF16),
             pltpu.VMEM((sections, order, width_y), BF16),
             pltpu.VMEM((order, order), F32),
             dma((sections,)), dma((8,)), dma((sections,)),

time: 20 us -> 19.5 us (0.975)
  the two profiles are of different devices: /device:TPU:19 before, /device:TPU:23 now
where the time goes in v3:
time: 19.5 us; the launch traced here: 19.4 us
  Pallas kernels  18.5 us (95%)
  other arithmetic  0.83 us (4%)
    pallas_call x1, Pallas kernels, per_device(): pl.pallas_call(functools.partial(kernel, sections, pair, 32), out_shape=p...  18.5 us
    broadcast_in_dim x1, other arithmetic, per_device(): return out.astype(F32)[None]  0.83 us

profile of v3, /device:TPU:23, one launch (start us, length us, event | category | flops | bytes accessed | tf_op | source)
XLA Modules:
  0.0 19.4 jit_solution(17209236458690998855)
XLA Ops:
  0.0 18.5 %shard_map.91 = bf16[1024,128]{1,0:T(8,128)(2,1)S(1)} custom-call(bf16[4,2,1024,128]{3,2,1,0:T(8,128)(2,1)} %recv_in.1, bf16[4,2,256]{2,1,0:T(2,128)(2,1)} %amp_in.1, s32[1,256]{1,0:T(1,128)} %bitcast.5, s32[1,256]{1,0:T(1,128)} %bitcast.6, f32[4]{0:T(128)} %omegas_in.1, f32[1,1024,128]{2,1,0:T(8,128)} %slow_in.1, bf16[4,4,2,256,256]{4,3,2,1,0:T(8,128)(2,1)} %table_in.1, ...), custom_call_target="tpu_custom_call" | custom-call | tf_op jit(solution)/shard_map/pallas_call | solution.py:432
  18.5 0.8 %bitcast_convert_fusion = f32[1,1024,128]{2,1,0:T(8,128)} fusion(bf16[1024,128]{1,0:T(8,128)(2,1)S(1)} %shard_map.91), kind=kLoop, calls=%fused_computation | loop fusion | flops 131072 | bytes 786432 | tf_op jit(solution)/shard_map/broadcast_in_dim | solution.py:476

commit v4 on v3

--- a/solution.py
+++ b/solution.py
@@ -51,9 +51,8 @@
     zones_x_in, zones_y_in,
     out, slow, slow_raw, code, rec, wave, table, forms, amp, src_x, src_y, omegas, zones_x, zones_y,
     zones, zone_buf, zone_rows, trig, rotated, inline, grad, got, total,
-    load_sems, local_sems, zone_sems, zone_send, zone_recv, slow_send, slow_recv, fwd_send, fwd_recv,
-    rec_send, rec_recv, swap_send, swap_recv, last_send, last_recv, grad_send, grad_recv, tail_send,
-    tail_recv, ready,
+    load_sems, local_sems, zone_send, zone_recv, slow_send, slow_recv, mate_send, fwd_recv,
+    rec_recv, swap_send, grad_send, grad_recv, ready,
 ):
     d = lax.axis_index("depth")
     line = lax.axis_index("xline")
@@ -64,7 +63,7 @@
     order = pair * width
     slots = wave.shape[0]
     last = sections - 1
-    parts = last_send.shape[0]
+    parts = PARTS
 
     def rows_of(section):
         return pl.ds(pl.multiple_of(section * order, order), order)
@@ -124,20 +123,20 @@
     for k, other in enumerate(others):
         zone_copies.append(
             pltpu.make_async_remote_copy(
-                src_ref=zones, dst_ref=zone_buf.at[d], send_sem=zone_send.at[k],
+                src_ref=zones, dst_ref=zone_buf.at[d], send_sem=zone_send,
                 recv_sem=zone_recv.at[d], device_id=(other, line), device_id_type=MESH,
             )
         )
         slow_copies.append(
             pltpu.make_async_remote_copy(
                 src_ref=code.at[rows_of(other), :], dst_ref=slow.at[d, q],
-                send_sem=slow_send.at[k], recv_sem=slow_recv.at[d],
+                send_sem=slow_send, recv_sem=slow_recv.at[d],
                 device_id=(other, line), device_id_type=MESH,
             )
         )
     rec_copy = pltpu.make_async_remote_copy(
         src_ref=recv_in.at[pl.ds((1 - q) * slots, slots), :, rows_of(d), :],
-        dst_ref=rec.at[q], send_sem=rec_send, recv_sem=rec_recv,
+        dst_ref=rec.at[q], send_sem=mate_send, recv_sem=rec_recv,
         device_id=(d, mate_line), device_id_type=MESH,
     )
 
@@ -147,12 +146,12 @@
 
     def arrived(level):
         zone = pltpu.make_async_remote_copy(
-            src_ref=zones, dst_ref=zone_buf.at[level], send_sem=zone_send.at[0],
+            src_ref=zones, dst_ref=zone_buf.at[level], send_sem=zone_send,
             recv_sem=zone_recv.at[level], device_id=(d, mate_line), device_id_type=MESH,
         )
         rest = pltpu.make_async_remote_copy(
             src_ref=slow.at[level, q], dst_ref=slow.at[level, q],
-            send_sem=slow_send.at[0], recv_sem=slow_recv.at[level],
+            send_sem=slow_send, recv_sem=slow_recv.at[level],
             device_id=(d, mate_line), device_id_type=MESH,
         )
         return zone, rest
@@ -160,13 +159,13 @@
     def forward(level, half):
         return pltpu.make_async_remote_copy(
             src_ref=slow.at[level, half], dst_ref=slow.at[level, half],
-            send_sem=fwd_send.at[level], recv_sem=fwd_recv.at[level],
+            send_sem=mate_send, recv_sem=fwd_recv.at[level],
             device_id=(d, mate_line), device_id_type=MESH,
         )
 
     def zone_copy(level):
         return pltpu.make_async_copy(
-            zone_buf.at[level], zone_rows.at[level], zone_sems.at[level]
+            zone_buf.at[level], zone_rows.at[level], load_sems.at[level]
         )
 
     def receive(level):
@@ -284,7 +283,7 @@
     def swap(level):
         return pltpu.make_async_remote_copy(
             src_ref=grad.at[level, 1 - q], dst_ref=got.at[level],
-            send_sem=swap_send.at[level], recv_sem=swap_recv.at[level],
+            send_sem=swap_send, recv_sem=local_sems.at[level],
             device_id=(d, mate_line), device_id_type=MESH,
         )
 
@@ -292,14 +291,14 @@
         part = pl.ds(k * (order // parts), order // parts)
         return pltpu.make_async_remote_copy(
             src_ref=grad.at[last, 1 - q, part], dst_ref=got.at[last, part],
-            send_sem=last_send.at[k], recv_sem=last_recv.at[k],
+            send_sem=swap_send, recv_sem=local_sems.at[last + k],
             device_id=(d, mate_line), device_id_type=MESH,
         )
 
     def deliver_copy(level):
         return pltpu.make_async_remote_copy(
             src_ref=got.at[level], dst_ref=out.at[rows_of(d), :],
-            send_sem=grad_send.at[level], recv_sem=grad_recv.at[d],
+            send_sem=grad_send, recv_sem=grad_recv,
             device_id=(level, line), device_id_type=MESH,
         )
 
@@ -311,7 +310,7 @@
         part = pl.ds(k * (order // parts), order // parts)
         return pltpu.make_async_remote_copy(
             src_ref=got.at[last, part], dst_ref=out.at[section_part(section, k), :],
-            send_sem=tail_send.at[k], recv_sem=tail_recv.at[section, k],
+            send_sem=grad_send, recv_sem=grad_recv,
             device_id=(last, line), device_id_type=MESH,
         )
 
@@ -383,36 +382,19 @@
     for k in range(parts):
         deliver_last(k)
 
-    for copy in zone_copies + slow_copies:
-        copy.wait_send()
-    rec_copy.wait_send()
-    for level in range(sections):
-        forward(level, q).wait_send()
-    for level in range(last):
-        swap(level).wait_send()
-
-        @pl.when(level != d)
-        def _():
-            deliver_copy(level).wait_send()
-    for k in range(parts):
-        swap_part(k).wait_send()
-
-    @pl.when(d != last)
-    def _():
-        for k in range(parts):
-            deliver_part(k, d).wait_send()
-        for other in others:
-            pltpu.make_async_remote_copy(
-                src_ref=got.at[0], dst_ref=out.at[rows_of(other), :],
-                send_sem=grad_send.at[0], recv_sem=grad_recv.at[other],
-                device_id=(d, mate_line), device_id_type=MESH,
-            ).wait_recv()
-
-    @pl.when(d == last)
-    def _():
-        for other in others:
-            for k in range(parts):
-                deliver_part(k, other).wait_recv()
+    def all_of(ref, send_sem, recv_sem):
+        return pltpu.make_async_remote_copy(
+            src_ref=ref, dst_ref=ref, send_sem=send_sem, recv_sem=recv_sem,
+            device_id=(d, mate_line), device_id_type=MESH,
+        )
+
+    all_of(zone_buf.at[pl.ds(0, last)], zone_send, grad_recv).wait_send()
+    all_of(code.at[pl.ds(0, last * order), :], slow_send, grad_recv).wait_send()
+    all_of(slow_raw, mate_send, grad_recv).wait_send()
+    all_of(grad.at[:, 0], swap_send, grad_recv).wait_send()
+    delivered = all_of(got.at[pl.ds(0, last)], grad_send, grad_recv)
+    delivered.wait_send()
+    delivered.wait_recv()
 
 
 def per_device(
@@ -425,7 +407,7 @@
     points = source_x.shape[0]
     zone_count = inverses.shape[1]
     slots = freqs // pair
-    assert pair == 2 and sections == 4 and width_x == order * sections and slowness.shape[0] == 1
+    assert slots * 2 == sections and pair == 2 and sections == 4 and width_x == order * sections and slowness.shape[0] == 1
     vmem = pl.BlockSpec(memory_space=pltpu.VMEM)
     anywhere = pl.BlockSpec(memory_space=pl.ANY)
     dma = pltpu.SemaphoreType.DMA
@@ -457,15 +439,9 @@
             pltpu.VMEM((sections, pair, order, width_y), BF16),
             pltpu.VMEM((sections, order, width_y), BF16),
             pltpu.VMEM((order, order), F32),
-            dma((sections,)), dma((8,)), dma((sections,)),
-            dma((sections,)), dma((sections,)),
-            dma((sections,)), dma((sections,)),
-            dma((sections,)), dma((sections,)),
-            dma, dma,
-            dma((sections,)), dma((sections,)),
-            dma((PARTS,)), dma((PARTS,)),
-            dma((sections,)), dma((sections,)),
-            dma((PARTS,)), dma((sections, PARTS)),
+            dma((sections,)), dma((8,)),
+            dma, dma((sections,)), dma, dma((sections,)),
+            dma, dma((sections,)), dma, dma, dma, dma,
             pltpu.SemaphoreType.REGULAR,
         ],
         compiler_params=pltpu.CompilerParams(collective_id=0, has_side_effects=True),

time: 19.5 us -> 19.2 us (0.985)
  Pallas kernels: 18.5 us -> 18.2 us
    pallas_call x1, Pallas kernels: 18.5 us -> 18.2 us  [per_device(): pl.pallas_call(functools.partial(kernel, sections, pair, 32), out_shape=p...]
where the time goes in v4:
time: 19.2 us; the launch traced here: 19 us
  Pallas kernels  18.2 us (95%)
  other arithmetic  0.83 us (4%)
    pallas_call x1, Pallas kernels, per_device(): pl.pallas_call(functools.partial(kernel, sections, pair, 32), out_shape=p...  18.2 us
    broadcast_in_dim x1, other arithmetic, per_device(): return out.astype(F32)[None]  0.83 us

profile of v4, /device:TPU:23, one launch (start us, length us, event | category | flops | bytes accessed | tf_op | source)
XLA Modules:
  0.0 19.0 jit_solution(14016260848702837486)
XLA Ops:
  0.0 18.2 %shard_map.91 = bf16[1024,128]{1,0:T(8,128)(2,1)S(1)} custom-call(bf16[4,2,1024,128]{3,2,1,0:T(8,128)(2,1)} %recv_in.1, bf16[4,2,256]{2,1,0:T(2,128)(2,1)} %amp_in.1, s32[1,256]{1,0:T(1,128)} %bitcast.5, s32[1,256]{1,0:T(1,128)} %bitcast.6, f32[4]{0:T(128)} %omegas_in.1, f32[1,1024,128]{2,1,0:T(8,128)} %slow_in.1, bf16[4,4,2,256,256]{4,3,2,1,0:T(8,128)(2,1)} %table_in.1, ...), custom_call_target="tpu_custom_call" | custom-call | tf_op jit(solution)/shard_map/pallas_call | solution.py:414
  18.2 0.8 %bitcast_convert_fusion = f32[1,1024,128]{2,1,0:T(8,128)} fusion(bf16[1024,128]{1,0:T(8,128)(2,1)S(1)} %shard_map.91), kind=kLoop, calls=%fused_computation | loop fusion | flops 131072 | bytes 786432 | tf_op jit(solution)/shard_map/broadcast_in_dim | solution.py:452
